TPU v7x, 32 devices: a whole 2x2x4 slice. The times are simulated.
32 devices in a mesh: ctx: 8 (over z, y), fsdp: 4 (over x, core).
Axes of the slice: x: 2, y: 2, z: 4, core: 2. Of those that a mesh axis runs over, the one named last changes fastest.
Arguments:
- hidden: bfloat16 [4096, 4096], P('ctx', 'fsdp'), may hold values from -6 to 6
- w_in: bfloat16 [768, 4096], P('ctx', 'fsdp'), may hold values from -1.25 to 1.25
- decay: float32 [4, 4096], P(None, 'ctx'), may hold values from 0.999 to 1
- norm_gain: float32 [256], replicated, may hold values from 0.1 to 1.9
- w_out: bfloat16 [256, 4096], P('ctx', 'fsdp'), may hold values from -0.75 to 0.75
- grad_out: bfloat16 [4096, 4096], P('ctx', 'fsdp'), may hold values from -6 to 6
Outputs:
- grad_hidden: bfloat16 [4096, 4096], P('ctx', 'fsdp')
- grad_w_in: float32 [768, 4096], P('ctx', 'fsdp')
- grad_w_out: float32 [256, 4096], P('ctx', 'fsdp')
All inputs are finite; a program needn't handle non-finite values.
Results may differ from a plain program's by a relative error of at most 0.0075.
Values may be sent and summed in bfloat16 or wider, within the bound.
A program may use at most 128 MiB of HBM per device.

v0:
```python
import math

import jax
import jax.numpy as jnp
from jax import lax
from jax.sharding import PartitionSpec as P

D = 4096
H = 4
P_SIZE = 64
N = 128
HP = 256


highest = lax.Precision.HIGHEST
clip_output = 10.0


def prefix(x, axis, combine, identity):
    count, index = (lax.axis_size(axis), lax.axis_index(axis))
    everything = jax.tree.map(lambda part: lax.all_gather(part, axis), x)
    start = jax.tree.map(
        lambda part, zero: jnp.broadcast_to(jnp.asarray(zero, part.dtype), part.shape), x, identity
    )

    def step(k, before):
        reached = k < index
        new = combine(before, jax.tree.map(lambda part: part[k], everything))
        return jax.tree.map(lambda a, b: jnp.where(reached, a, b), new, before)

    return lax.fori_loop(0, count, step, start)


def entering(x, axis, join, neutral):
    count = lax.axis_size(axis)
    place = lax.axis_index(axis)
    ahead = count - 1 - place
    gathered = jax.tree.map(
        lambda a, kind: lax.all_gather(a.astype(kind), axis),
        x,
        jax.tree.map(lambda a: jnp.bfloat16 if a.dtype == jnp.float32 else a.dtype, x),
    )
    state = jax.tree.map(lambda a, e: jnp.zeros_like(a) + jnp.asarray(e, a.dtype), x, neutral)

    def one(step, state):
        source = count - 1 - step
        return join(
            state,
            jax.tree.map(
                lambda a, own: lax.dynamic_index_in_dim(a, source, 0, False).astype(own.dtype),
                gathered,
                x,
            ),
        )

    return lax.fori_loop(0, ahead, one, state)


def split_columns(projection):
    return (
        projection[:, :HP],
        projection[:, HP : 2 * HP],
        projection[:, 2 * HP : 2 * HP + N],
        projection[:, 2 * HP + N :],
    )


def intra_block(x_part, b_part, c_part, log_decay):
    length = x_part.shape[0]
    cum_decay = jnp.cumsum(log_decay, axis=1)
    x_heads = x_part.reshape(length, H, P_SIZE)
    causal = jnp.arange(length)[:, None] >= jnp.arange(length)[None, :]
    gaps = jnp.where(causal[None], cum_decay[:, :, None] - cum_decay[:, None, :], 0.0)
    weights = jnp.where(causal[None], jnp.exp(gaps), 0.0)
    scores = jnp.dot(c_part, b_part.T, precision=highest)
    mixed = weights * scores[None]
    y_intra = jnp.einsum("hts,shp->thp", mixed, x_heads, precision=highest).reshape(
        length, H * P_SIZE
    )
    tail = jnp.exp(cum_decay[:, -1:] - cum_decay)
    weighted = x_heads * tail.T[:, :, None]
    state_part = jnp.einsum("shp,sn->hpn", weighted, b_part, precision=highest)
    return (y_intra, state_part, cum_decay)


def finish_block(gate_part, y_intra, c_part, start_state, cum_decay, norm_gain):
    length = c_part.shape[0]
    carried = jnp.einsum("hpn,tn->thp", start_state, c_part, precision=highest)
    carried = carried * jnp.exp(cum_decay).T[:, :, None]
    y_full = y_intra + carried.reshape(length, H * P_SIZE)
    gated = y_full * jax.nn.silu(gate_part)
    factor = lax.rsqrt(jnp.mean(gated * gated, axis=-1, keepdims=True) + 1e-05)
    return gated * factor * norm_gain


def carry_states(earlier, later):
    return (earlier[0] * later[0], later[0] * earlier[1] + later[1])


def carry_adjoint(earlier, later):
    return (earlier[0] * later[0], later[1] + later[0] * earlier[1])


def local(hidden, w_in, decay, norm_gain, w_out, grad_out):
    clip_input = math.sqrt(D)
    tok_rows = hidden.shape[0]
    root_tokens = math.sqrt(tok_rows * lax.axis_size("ctx"))
    contract_last = (((1,), (1,)), ((), ()))
    contract_first = (((0,), (0,)), ((), ()))
    partial_proj = lax.dot_general(
        hidden,
        lax.all_gather(w_in, "ctx", axis=0, tiled=True),
        contract_last,
        preferred_element_type=jnp.float32,
    )
    slab_out = lax.all_gather(w_out, "ctx", axis=0, tiled=True)
    partial_grad = lax.dot_general(
        grad_out, slab_out, contract_last, preferred_element_type=jnp.float32
    )
    projection, grad_normed = lax.psum((partial_proj, partial_grad), "fsdp")
    log_decay = jnp.log(decay)
    gate_part, x_part, b_part, c_part = split_columns(projection)

    def intra_only(x_value, b_value, c_value):
        return intra_block(x_value, b_value, c_value, log_decay)

    (y_intra, state_part, cum_decay), intra_pull = jax.vjp(intra_only, x_part, b_part, c_part)
    decay_total = jnp.exp(cum_decay[:, -1])[:, None, None]
    identity = (jnp.ones_like(decay_total), jnp.zeros_like(state_part))
    _, start_state = prefix((decay_total, state_part), "ctx", carry_states, identity)

    def finish_only(gate_value, intra_value, c_value, state_value):
        return finish_block(gate_value, intra_value, c_value, state_value, cum_decay, norm_gain)

    normed, finish_pull = jax.vjp(finish_only, gate_part, y_intra, c_part, start_state)
    grad_gate, grad_intra, grad_c_late, grad_start = finish_pull(grad_normed)
    _, grad_end = entering((decay_total, grad_start), "ctx", carry_adjoint, identity)
    grad_x, grad_b, grad_c_early = intra_pull((grad_intra, grad_end, jnp.zeros_like(cum_decay)))
    grad_projection = jnp.concatenate(
        [grad_gate, grad_x, grad_b, grad_c_early + grad_c_late], axis=1
    ).astype(jnp.bfloat16)
    columns = grad_projection
    grad_hidden = jnp.dot(
        columns, lax.all_gather(w_in, "ctx", axis=0, tiled=True), preferred_element_type=jnp.float32
    )
    columns = grad_projection
    raw_in = (
        lax.psum_scatter(
            lax.dot_general(columns, hidden, contract_first, preferred_element_type=jnp.float32),
            "ctx",
            scatter_dimension=0,
            tiled=True,
        )
        / root_tokens
    )
    weight_square = jnp.sum(jnp.square(w_in.astype(jnp.float32)), axis=1)
    weight_in, grad_in = lax.psum((weight_square, jnp.sum(raw_in * raw_in, axis=1)), "fsdp")
    factor_in = jnp.minimum(
        1.0,
        clip_input
        * jnp.maximum(jnp.sqrt(weight_in), 0.001)
        / jnp.maximum(jnp.sqrt(grad_in), 1e-06),
    )
    normed_rounded = normed.astype(jnp.bfloat16)
    weight_out = jnp.sqrt(jnp.sum(jnp.square(slab_out.astype(jnp.float32)), axis=0))
    raw_out = (
        lax.psum_scatter(
            lax.dot_general(
                normed_rounded, grad_out, contract_first, preferred_element_type=jnp.float32
            ),
            "ctx",
            scatter_dimension=0,
            tiled=True,
        )
        / root_tokens
    )
    grad_square = lax.psum(jnp.sum(raw_out * raw_out, axis=0), "ctx")
    factor_out = jnp.minimum(
        1.0,
        clip_output * jnp.maximum(weight_out, 0.001) / jnp.maximum(jnp.sqrt(grad_square), 1e-06),
    )
    return (
        grad_hidden.astype(jnp.bfloat16),
        raw_in * factor_in[:, None],
        raw_out * factor_out[None, :],
    )


def solution(mesh):
    return jax.shard_map(
        local,
        mesh=mesh,
        in_specs=(
            P("ctx", "fsdp"),
            P("ctx", "fsdp"),
            P(None, "ctx"),
            P(),
            P("ctx", "fsdp"),
            P("ctx", "fsdp"),
        ),
        out_specs=(P("ctx", "fsdp"), P("ctx", "fsdp"), P("ctx", "fsdp")),
        check_vma=False,
    )
```

profile of v0, /device:TPU:0, one launch (start us, length us, event | category | flops | bytes accessed | tf_op | source)
XLA Modules:
  0.0 381.3 jit_solution(6194710218031566546)
XLA Ops:
  7.2 0.7 all-gather.7.cloned.1.call-update
  8.0 33.8 %all_gather.30 = bf16[256,1024]{1,0:T(8,128)(2,1)S(1)} all-gather(bf16[32,1024]{1,0:T(8,128)(2,1)} %param.14), channel_id=1, replica_groups=mesh['ctx'=8,'fsdp'=4] {'ctx'}, dimensions={0}, use_global_device_ids=true | all-gather | bytes 589824 | tf_op jit(solution)/shard_map/all_gather | solution.py:116
  41.8 0.8 copy-done.3
  42.6 2.5 fusion.66
  45.1 12.9 %all-gather.7.cloned.1.call-done = bf16[768,1024]{1,0:T(8,128)(2,1)} async-done(((bf16[96,1024]{1,0:T(8,128)(2,1)}), bf16[768,1024]{1,0:T(8,128)(2,1)}) %all-gather.7.cloned.1.call-update) | async-done | bytes 1572880 | tf_op jit(solution)/shard_map/all_gather | solution.py:112
  58.0 3.6 fusion.65
  61.7 0.6 copy-done.14
  62.3 1.2 reduce-window.6
  64.2 47.7 %all-reduce.6.cloned.1.call-done = (f32[512,768]{1,0:T(8,128)}, f32[512,256]{1,0:T(8,128)}) async-done(((f32[512,768]{1,0:T(8,128)}, f32[512,256]{1,0:T(8,128)}), (f32[512,768]{1,0:T(8,128)}, f32[512,256]{1,0:T(8,128)})) %all-reduce.6.cloned.1.call-update) | async-done | bytes 2097168 | tf_op jit(solution)/shard_map/psum | solution.py:120
  111.9 2.0 slice.29
  113.8 1.2 copy.35
  115.1 1.2 fusion.34
  116.4 0.6 dynamic-slice
  117.7 0.2 dynamic-update-slice.1
  117.9 21.4 %all-reduce.1 = bf16[32]{0:T(256)(128)(2,1)S(1)} all-reduce(bf16[32]{0:T(256)(128)(2,1)S(1)} %dynamic-update-slice.1), channel_id=5, replica_groups=mesh['ctx'=8,'fsdp'=4] {'ctx'}, use_global_device_ids=true, to_apply=%add.1 | all-reduce | flops 32 | bytes 128
  139.5 17.6 %all-reduce = f32[32]{0:T(128)S(1)} all-reduce(f32[32]{0:T(128)S(1)} %bitcast_dynamic-update-slice_fusion), channel_id=2, replica_groups=mesh['ctx'=8,'fsdp'=4] {'ctx'}, use_global_device_ids=true, to_apply=%add | all-reduce | flops 32 | bytes 256
  157.3 1.0 fusion.51
  158.3 1.0 copy-done.7
  159.3 5.9 %fusion.16 = f32[512,4,64]{0,2,1:T(8,128)} fusion(f32[512,4,64]{0,2,1:T(8,128)S(1)} %bitcast.85, f32[512,512]{1,0:T(8,128)S(1)} %fusion.51, f32[4,512]{1,0:T(4,128)S(1)} %bitcast.97, pred[512,512]{1,0:T(8,128)(4,1)S(1)} %iota_compare_fusion), kind=kOutput, calls=%fused_computation.21 | convolution fusion | flops 809500672 | bytes 2367488 | tf_op jit(solution)/shard_map/jvp(hts,shp->thp)/dot_general | solution.py:77
  165.2 8.2 %while.29 = (s32[]{:T(128)}, f32[4,64,128]{2,1,0:T(8,128)S(1)}, s32[]{:T(128)}, f32[8,4,1,1]{1,3,2,0:T(1,128)S(1)}, f32[8,4,64,128]{3,2,1,0:T(8,128)}, /*index=5*/s32[]{:T(128)}, s32[]{:T(128)}) while((s32[]{:T(128)}, f32[4,64,128]{2,1,0:T(8,128)S(1)}, s32[]{:T(128)}, f32[8,4,1,1]{1,3,2,0:T(1,128)S(1)}, ...), condition=%wide.region_4.5_spmd.clone, body=%wide.region_3.4_spmd.clone.sunk | while | flops 131076 | bytes 393377 | solution.py:31
  165.2 1.0 fusion.85
  166.2 1.0 fusion.85
  167.2 1.0 fusion.85
  168.3 1.0 fusion.85
  169.3 1.0 fusion.85
  170.3 1.0 fusion.85
  171.4 1.0 fusion.85
  172.4 1.0 fusion.85
  173.4 2.5 fusion.23
  175.9 2.1 copy.39
  177.9 1.6 multiply_reduce_fusion.3
  179.6 0.8 copy-done.5
  180.3 1.6 fusion.36
  181.9 2.6 fusion.29
  184.5 2.0 copy.40
  186.5 1.6 convolution_convert_fusion.1
  188.2 33.5 %all-gather.2 = bf16[32,64,128]{2,1,0:T(8,128)(2,1)} all-gather(bf16[4,64,128]{2,1,0:T(8,128)(2,1)S(1)} %convolution_convert_fusion.1), channel_id=4, replica_groups=mesh['ctx'=8,'fsdp'=4] {'ctx'}, dimensions={0}, use_global_device_ids=true | all-gather | bytes 589824 | tf_op jit(solution)/shard_map/all_gather | solution.py:39
  221.7 6.8 %while.28 = (s32[]{:T(128)}, f32[4,64,128]{2,1,0:T(8,128)S(1)}, s32[]{:T(128)}, bf16[8,4,64,128]{3,2,1,0:T(8,128)(2,1)}, bf16[8,4,1,1]{1,3,2,0:T(2,128)(2,1)S(1)...) while((s32[]{:T(128)}, f32[4,64,128]{2,1,0:T(8,128)S(1)}, s32[]{:T(128)}, ...), condition=%wide.region_9.10_spmd, body=%wide.region_8.9_spmd.sunk | while | flops 98314 | bytes 327875 | solution.py:56
  221.7 0.9 convert_add_fusion.2
  222.7 0.9 convert_add_fusion.2
  223.6 0.9 convert_add_fusion.2
  224.6 0.9 convert_add_fusion.2
  225.6 0.9 convert_add_fusion.2
  226.6 0.9 convert_add_fusion.2
  227.5 0.9 convert_add_fusion.2
  228.7 5.2 %fusion.19 = f32[512,4,64]{0,2,1:T(8,128)S(1)} fusion(f32[4,64,512]{2,1,0:T(8,128)} %bitcast.89, f32[512,512]{1,0:T(8,128)} %copy-done.7, f32[4,512]{1,0:T(4,128)S(1)} %bitcast.98, pred[512,512]{1,0:T(8,128)(4,1)} %copy-done.9), kind=kOutput, calls=%fused_computation.22 | convolution fusion | flops 809500672 | bytes 2367488 | tf_op jit(solution)/shard_map/transpose(jvp(hts,shp->thp))/dot_general | solution.py:77
  234.0 1.3 fusion.24
  235.3 1.8 copy.46
  237.1 2.1 convolution_bitcast_fusion
  239.2 1.0 convolution_bitcast_fusion.1
  240.2 5.1 %multiply_reduce_fusion = f32[512,512]{1,0:T(8,128)S(1)} fusion(f32[4,64,512]{2,1,0:T(8,128)S(1)} %bitcast.91, f32[512,4,64]{0,2,1:T(8,128)S(1)} %bitcast.87, f32[4,512]{1,0:T(4,128)S(1)} %bitcast.99, pred[512,512]{1,0:T(8,128)(4,1)S(1)} %copy-done.10), kind=kOutput, calls=%fused_computation.5 | convolution fusion | flops 810287104 | bytes 2367488 | tf_op jit(solution)/shard_map/transpose(jvp(hts,shp->thp))/dot_general | solution.py:77
  245.4 1.0 fusion.26
  246.4 1.8 fusion.25
  248.2 2.7 fusion.57
  250.9 0.9 copy-done.8
  252.2 3.4 convolution_convert_fusion
  255.5 33.2 %reduce-scatter.5.cloned.1.call-done = f32[32,1024]{1,0:T(8,128)} async-done(((f32[256,1024]{1,0:T(8,128)}), f32[32,1024]{1,0:T(8,128)}) %reduce-scatter.5.cloned.1.call-update) | async-done | bytes 131088 | tf_op jit(solution)/shard_map/reduce_scatter | solution.py:167
  288.7 0.9 multiply_reduce_fusion.6
  289.6 19.8 %psum.39 = f32[1024]{0:T(1024)S(1)} all-reduce(f32[1024]{0:T(1024)S(1)} %multiply_reduce_fusion.6), channel_id=1, replica_groups=mesh['ctx'=8,'fsdp'=4] {'ctx'}, use_global_device_ids=true, to_apply=%region_19.20 | all-reduce | flops 1024 | bytes 8192 | tf_op jit(solution)/shard_map/psum | solution.py:177
  309.5 1.6 broadcast_multiply_fusion.1
  311.0 54.6 %reduce-scatter.3.cloned.1.call-done = f32[96,1024]{1,0:T(8,128)} async-done(((f32[768,1024]{1,0:T(8,128)}), f32[96,1024]{1,0:T(8,128)}) %reduce-scatter.3.cloned.1.call-update) | async-done | bytes 393232 | tf_op jit(solution)/shard_map/reduce_scatter | solution.py:148
  365.7 1.1 multiply_reduce_fusion.4
  366.8 6.1 %all-reduce.2 = (f32[96]{0:T(128)S(1)}, f32[96]{0:T(128)S(1)}) all-reduce(f32[96]{0:T(128)S(1)} %multiply_reduce_fusion.4, f32[96]{0:T(128)S(1)} %multiply_reduce_fusion.5), channel_id=1, replica_groups=mesh['ctx'=8,'fsdp'=4] {'fsdp'}, use_global_device_ids=true, to_apply=%region_15.16 | all-reduce | flops 192 | bytes 1536 | tf_op jit(solution)/shard_map/psum | solution.py:157
  372.9 1.8 broadcast_multiply_fusion
  (75 shorter events, 2.1 us)
Async XLA Ops:
  7.2 50.8 %copy-start = (bf16[512,1024]{1,0:T(8,128)(2,1)S(1)}, bf16[512,1024]{1,0:T(8,128)(2,1)}, u32[]{:S(2)}) copy-start(bf16[512,1024]{1,0:T(8,128)(2,1)} %param.10) | copy-start | bytes 3145732
  7.2 50.8 %all-gather.7.cloned.1.call-start = ((), (), s32[]{:S(2)}) async-start(), calls=%async_computation.2 | async-start | bytes 1769472 | tf_op jit(solution)/shard_map/all_gather | solution.py:112
  7.9 103.9 %all-reduce.6.cloned.1.call-start = ((), (), s32[]{:S(2)}) async-start(), calls=%async_computation.6 | async-start | bytes 4194304 | tf_op jit(solution)/shard_map/psum | solution.py:120
  41.8 0.8 copy-start.3
  61.6 0.7 copy-start.14
  61.6 103.5 %all-gather.9.cloned.1.call-start = ((), (), s32[]{:S(2)}) async-start(), calls=%async_computation.5 | async-start | bytes 1179648 | tf_op jit(solution)/shard_map/all_gather | solution.py:21
  111.9 3.2 copy-start.1
  111.9 4.6 %copy-start.15 = (u32[32]{0:T(128)S(1)}, u32[32]{0:T(128)}, u32[]{:S(2)}) copy-start(u32[32]{0:T(128)} %constant.101) | copy-start | bytes 388
  116.4 172.4 %reduce-scatter.5.cloned.1.call-start = ((), (), s32[]{:S(2)}) async-start(), calls=%async_computation.4 | async-start | bytes 1179648 | tf_op jit(solution)/shard_map/reduce_scatter | solution.py:167
  157.3 1.0 copy-start.9
  158.3 1.0 copy-start.7
  173.4 4.5 %copy-start.13 = (f32[256]{0:T(256)S(1)}, f32[256]{0:T(256)}, u32[]{:S(2)}) copy-start(f32[256]{0:T(256)} %param.13) | copy-start | bytes 3076
  177.9 2.4 copy-start.6
  179.5 0.8 copy-start.5
  228.5 137.2 %reduce-scatter.3.cloned.1.call-start = ((), (), s32[]{:S(2)}) async-start(), calls=%async_computation.3 | async-start | bytes 3538944 | tf_op jit(solution)/shard_map/reduce_scatter | solution.py:148
  237.1 3.1 copy-start.2
  237.1 3.1 copy-start.10
  245.3 2.9 copy-start.11
  245.3 2.9 copy-start.12
  250.9 0.9 copy-start.8
  250.9 1.2 copy-start.4
Sparse Core Ops, SparseCore 0:
  10.2 47.7 all-gather.6
  61.7 50.0 all-reduce.5
  116.5 40.6 all-gather.8
  228.6 60.0 reduce-scatter.4
  292.1 73.4 reduce-scatter.2
where the time goes:
time: 383 us; the launch traced here: 381 us
  waiting for transfers between devices  149 us (39%)
  blocking collectives  132 us (34%)
  matrix products  43.5 us (11%)
  other arithmetic  26.1 us (7%)
  local copies, waits for them, and re-layouts  14.8 us (4%)
  between operations  14.7 us (4%)
    reduce_scatter x1, waiting for transfers between devices, local(): lax.psum_scatter(lax.dot_general(columns, hidden, contract_first, preferr...  54.6 us
    psum x1, waiting for transfers between devices, local(): projection, grad_normed = lax.psum((partial_proj, partial_grad), 'fsdp')  47.7 us
    unnamed x2, blocking collectives  39 us
    all_gather x1, blocking collectives, local(): slab_out = lax.all_gather(w_out, 'ctx', axis=0, tiled=True)  33.8 us
    all_gather x1, blocking collectives, entering(): lax.all_gather(a.astype(kind), axis)  33.5 us
    reduce_scatter x1, waiting for transfers between devices, local(): lax.psum_scatter(lax.dot_general(normed_rounded, grad_out, contract_first...  33.2 us
    psum x1, blocking collectives, local(): grad_square = lax.psum(jnp.sum(raw_out * raw_out, axis=0), 'ctx')  19.8 us
    dot_general x3, matrix products, intra_block(): jnp.einsum('hts,shp->thp', mixed, x_heads, precision=highest)  16.2 us
  transfers between devices with their start and end apart: 5, of which 4 were waited for; matrix products, arithmetic and copies ran while one was open for 11% of the time, Pallas kernels for 0%

commit v1 on v0

--- a/solution.py
+++ b/solution.py
@@ -1,8 +1,11 @@
+import functools
 import math
 
 import jax
 import jax.numpy as jnp
 from jax import lax
+from jax.experimental import pallas as pl
+from jax.experimental.pallas import tpu as pltpu
 from jax.sharding import PartitionSpec as P
 
 D = 4096
@@ -186,9 +189,370 @@
     )
 
 
+NN = (((1,), (0,)), ((), ()))
+NT = (((1,), (1,)), ((), ()))
+TN = (((0,), (0,)), ((), ()))
+MESH = pl.DeviceIdType.MESH
+f32 = jnp.float32
+bf16 = jnp.bfloat16
+EPS = 1e-05
+PARTS = 4
+
+
+def split(a):
+    hi = a.astype(bf16)
+    return hi, (a - hi.astype(f32)).astype(bf16)
+
+
+def dot1(a, b, dims):
+    return lax.dot_general(a, b, dims, preferred_element_type=f32)
+
+
+def dot3(a, b, dims):
+    return dot1(a[0], b[0], dims) + (dot1(a[0], b[1], dims) + dot1(a[1], b[0], dims))
+
+
+def transposed(pair):
+    return pair[0].T, pair[1].T
+
+
+def fused(
+    n, fs, root_tokens, clip_input,
+    hid_ref, win_ref, dec_ref, gain_ref, wout_ref, gout_ref,
+    gh_ref, gwi_ref, gwo_ref,
+    hidT, goutT, wi_all, wo_all, pT, core_in, x_out, x_in,
+    e_ref, st_out, st_all, s0_ref, ad_out, ad_all, g_ref,
+    ro, ob1, ob1r, ob2, ob2r, gp, ri, ib1, ib1r, ib2, ib2r,
+    nin_out, nin_all, nout_out, nout_all,
+    g_send, g_recv, p_send, p_recv, s_send, s_recv, o_send, o_recv, i_send, i_recv,
+    n_send, n_recv, tmp, c_in,
+):
+    c = lax.axis_index("ctx")
+    f = lax.axis_index("fsdp")
+    outer = n // 2
+    z, y = c // 2, lax.rem(c, 2)
+    yn = c + 1 - 2 * y
+    core = lax.rem(f, 2)
+    fcore = f + 1 - 2 * core
+    fx = lax.rem(f + fs // 2, fs)
+    rows_in, d = win_ref.shape
+    rows_out = wout_ref.shape[0]
+    tok = hid_ref.shape[0]
+    cin, hp = rows_in * n, rows_out * n
+    nst = (cin - 2 * hp) // 2
+    hpf = hp // fs
+
+    def copy(src, dst, ssem, rsem, dev):
+        return pltpu.make_async_remote_copy(
+            src_ref=src, dst_ref=dst, send_sem=ssem, recv_sem=rsem,
+            device_id=dev, device_id_type=MESH)
+
+    sent = []
+
+    def go(*args):
+        made = copy(*args)
+        made.start()
+        sent.append(made)
+        return made
+
+    barrier = pltpu.get_barrier_semaphore()
+    for k in range(1, n):
+        pl.semaphore_signal(barrier, inc=1, device_id=(lax.rem(c + k, n), f), device_id_type=MESH)
+    for k in range(1, fs):
+        pl.semaphore_signal(barrier, inc=1, device_id=(c, lax.rem(f + k, fs)), device_id_type=MESH)
+    pl.semaphore_wait(barrier, n + fs - 2)
+
+    both = ((win_ref, wi_all), (wout_ref, wo_all))
+    for a, (src, dst) in enumerate(both):
+        go(src, dst.at[c], g_send.at[a, 0], g_recv.at[a, c], (yn, f))
+    order = [1, outer - 1] + list(range(2, outer - 1))
+    for k in order:
+        peer = lax.rem(z + k, outer) * 2 + y
+        for a, (src, dst) in enumerate(both):
+            go(src, dst.at[c], g_send.at[a, k], g_recv.at[a, c], (peer, f))
+    wi_all[c] = win_ref[...]
+    wo_all[c] = wout_ref[...]
+    hidT[...] = hid_ref[...].T
+    goutT[...] = gout_ref[...].T
+
+    decay = dec_ref[...]
+    lane = lax.broadcasted_iota(jnp.int32, decay.shape, 1)
+    shift = 1
+    while shift < tok:
+        decay = decay * jnp.where(lane >= shift, pltpu.roll(decay, shift, 1), 1.0)
+        shift *= 2
+    heads = decay.shape[0]
+    for h in range(heads):
+        e_ref[h * (hp // heads) : (h + 1) * (hp // heads), :] = jnp.broadcast_to(
+            decay[h : h + 1], (hp // heads, tok))
+
+    def project(s):
+        pT[pl.ds(pl.multiple_of(s * rows_in, 8), rows_in), :] = dot1(wi_all[s], hidT[...], NN)
+        pT[pl.ds(pl.multiple_of(cin + s * rows_out, 8), rows_out), :] = dot1(
+            wo_all[s], goutT[...], NN)
+
+    project(c)
+    for k in order:
+        s = lax.rem(z + outer - k, outer) * 2 + y
+        for a, (src, dst) in enumerate(both):
+            copy(src, dst.at[s], g_send.at[a, k], g_recv.at[a, s], (yn, f)).wait_recv()
+            go(dst.at[s], dst.at[s], g_send.at[a, outer + k], g_recv.at[a, s], (yn, f))
+        project(s)
+    for k in [0] + order:
+        s = lax.rem(z + outer - k, outer) * 2 + 1 - y
+        for a, (src, dst) in enumerate(both):
+            copy(src, dst.at[s], g_send.at[a, 0], g_recv.at[a, s], (yn, f)).wait_recv()
+        project(s)
+
+    half = (cin + hp) // 2
+    size = half // PARTS
+    first = []
+    for j in range(PARTS):
+        part = pl.ds(pl.multiple_of((1 - core) * half + j * size, 8), size)
+        first.append(copy(pT.at[part], core_in.at[j], p_send.at[0, j], p_recv.at[0, j], (c, fcore)))
+        first[j].start()
+    mine = [pl.ds(pl.multiple_of(core * half + j * size, 8), size) for j in range(PARTS)]
+    for j in range(PARTS):
+        copy(core_in.at[j], core_in.at[j], p_send.at[0, j], p_recv.at[0, j], (c, fcore)).wait_recv()
+        total = pT[mine[j], :] + core_in[j]
+        pT[mine[j], :] = total
+        x_out[j] = total.astype(bf16)
+        go(x_out.at[j], x_in.at[j], p_send.at[1, j], p_recv.at[1, j], (c, fx))
+    for j in range(PARTS):
+        copy(x_out.at[j], x_in.at[j], p_send.at[1, j], p_recv.at[1, j], (c, fx)).wait_recv()
+        pT[mine[j], :] = pT[mine[j], :] + x_in[j].astype(f32)
+        go(pT.at[mine[j]], c_in.at[j], p_send.at[2, j], p_recv.at[2, j], (c, fcore))
+    for j in range(PARTS):
+        first[j].wait_send()
+    for j in range(PARTS):
+        part = pl.ds(pl.multiple_of((1 - core) * half + j * size, 8), size)
+        copy(c_in.at[j], c_in.at[j], p_send.at[2, j], p_recv.at[2, j], (c, fcore)).wait_recv()
+        pT[part, :] = c_in[j]
+
+    e = e_ref[...]
+    einv = 1.0 / e
+    eend = e[:, tok - 1 : tok]
+    gate = pT[:hp, :]
+    xs = pT[hp : 2 * hp, :] * einv
+    bT = pT[2 * hp : 2 * hp + nst, :]
+    cT = pT[2 * hp + nst : cin, :]
+    xs2, b2, c2 = split(xs), split(bT), split(cT)
+    tmp[...] = dot3(xs2, b2, NT) * eend
+    own = pl.ds(pl.multiple_of(f * hpf, 8), hpf)
+    st_out[:hpf, :] = tmp[own, :]
+    last = e_ref[pl.ds(pl.multiple_of(f * hpf, 8), 8), tok - 128 : tok]
+    st_out[hpf:, :] = jnp.broadcast_to(last[:, 127:128], (8, nst))
+    for k in range(1, n):
+        go(st_out, st_all.at[c], s_send.at[0, k], s_recv.at[0, c], (lax.rem(c + k, n), f))
+    st_all[c] = st_out[...]
+
+    upper = lax.broadcasted_iota(jnp.int32, (tok, tok), 0) <= lax.broadcasted_iota(
+        jnp.int32, (tok, tok), 1)
+    scores2 = split(jnp.where(upper, dot3(transposed(b2), c2, NN), 0.0))
+    y_in = dot3(xs2, scores2, NN)
+    sig = 1.0 / (1.0 + jnp.exp(-gate))
+    silu = gate * sig
+
+    for k in range(1, n):
+        s = lax.rem(c + n - k, n)
+        copy(st_out, st_all.at[s], s_send.at[0, k], s_recv.at[0, s], (s, f)).wait_recv()
+    state = jnp.zeros((hpf, nst), f32)
+    for k in range(n - 1):
+        new = st_all[k, hpf : hpf + 1, :] * state + st_all[k, :hpf, :]
+        state = jnp.where(k < c, new, state)
+    s0_ref[own, :] = state
+    for k in range(1, fs):
+        go(s0_ref.at[own], s0_ref.at[own], s_send.at[1, k], s_recv.at[1, f], (c, lax.rem(f + k, fs)))
+    for k in range(1, fs):
+        p = lax.rem(f + fs - k, fs)
+        rows = pl.ds(pl.multiple_of(p * hpf, 8), hpf)
+        copy(s0_ref.at[rows], s0_ref.at[rows], s_send.at[1, k], s_recv.at[1, p], (c, p)).wait_recv()
+    s02 = split(s0_ref[...])
+    yT = (y_in + dot3(s02, c2, NN)) * e
+
+    gain = gain_ref[...]
+    gated = yT * silu
+    r = lax.rsqrt(jnp.mean(gated * gated, axis=0, keepdims=True) + EPS)
+    normed = (gated * r * gain).astype(bf16)
+    u = pT[cin:, :] * gain
+    dgated = r * u - gated * (r * r * r * jnp.mean(u * gated, axis=0, keepdims=True))
+    dys2 = split(dgated * silu * e)
+    tmp[...] = dot3(dys2, c2, NT)
+    ad_out[...] = tmp[own, :].astype(bf16)
+    for k in range(1, n):
+        go(ad_out, ad_all.at[c], s_send.at[2, k], s_recv.at[2, c], (lax.rem(c + k, n), f))
+    ad_all[c] = ad_out[...]
+    gp[:hp, :] = (dgated * yT * (sig * (1.0 + gate * (1.0 - sig)))).astype(bf16)
+
+    ro[...] = dot1(normed, gout_ref[...], NN)
+    for q in range(outer):
+        at = pl.ds(pl.multiple_of((q * 2 + 1 - y) * rows_out, 8), rows_out)
+        ob1[q] = ro[at, :].astype(bf16)
+    go(ob1, ob1r, o_send.at[0], o_recv.at[0], (yn, f))
+
+    dscores2 = split(jnp.where(upper, dot3(transposed(xs2), dys2, NN), 0.0))
+    gp[2 * hp + nst :, :] = (dot3(b2, dscores2, NN) + dot3(transposed(s02), dys2, NN)).astype(bf16)
+    db = dot3(c2, dscores2, NT)
+    dxs = dot3(dys2, scores2, NT)
+
+    copy(ob1, ob1r, o_send.at[0], o_recv.at[0], (yn, f)).wait_recv()
+    for q in range(outer):
+        at = pl.ds(pl.multiple_of((q * 2 + y) * rows_out, 8), rows_out)
+        total = ro[at, :] + ob1r[q].astype(f32)
+        ro[at, :] = total
+        ob2[q] = total.astype(bf16)
+
+    for k in range(1, n):
+        s = lax.rem(c + n - k, n)
+        copy(ad_out, ad_all.at[s], s_send.at[2, k], s_recv.at[2, s], (s, f)).wait_recv()
+    adj = jnp.zeros((hpf, nst), f32)
+    for k in range(n - 1, 0, -1):
+        new = st_all[k, hpf : hpf + 1, :] * adj + ad_all[k].astype(f32)
+        adj = jnp.where(k > c, new, adj)
+    g_ref[own, :] = adj
+    for k in range(1, fs):
+        go(g_ref.at[own], g_ref.at[own], s_send.at[3, k], s_recv.at[3, f], (c, lax.rem(f + k, fs)))
+    for k in range(1, outer):
+        q = lax.rem(z + k, outer)
+        go(ob2.at[q], ob2r.at[z], o_send.at[k], o_recv.at[1 + z], (q * 2 + y, f))
+    for k in range(1, fs):
+        p = lax.rem(f + fs - k, fs)
+        rows = pl.ds(pl.multiple_of(p * hpf, 8), hpf)
+        copy(g_ref.at[rows], g_ref.at[rows], s_send.at[3, k], s_recv.at[3, p], (c, p)).wait_recv()
+    g2 = split(g_ref[...] * eend)
+    gp[hp : 2 * hp, :] = ((dxs + dot3(g2, b2, NN)) * einv).astype(bf16)
+    gp[2 * hp : 2 * hp + nst, :] = (db + dot3(transposed(g2), xs2, NN)).astype(bf16)
+
+    def rows_of(s):
+        return pl.ds(pl.multiple_of(s * rows_in, 16), rows_in)
+
+    far = order[::-1] + [0]
+    for i, k in enumerate(far):
+        q = lax.rem(z + k, outer)
+        ib1[i] = dot1(gp[rows_of(q * 2 + 1 - y), :], hid_ref[...], NN).astype(bf16)
+        go(ib1.at[i], ib1r.at[i], i_send.at[0, i], i_recv.at[0, i], (yn, f))
+    for i, k in enumerate(far):
+        q = lax.rem(z + k, outer)
+        part = dot1(gp[rows_of(q * 2 + y), :], hid_ref[...], NN)
+        copy(ib1.at[i], ib1r.at[i], i_send.at[0, i], i_recv.at[0, i], (yn, f)).wait_recv()
+        part = part + ib1r[i].astype(f32)
+        if k:
+            ib2[i] = part.astype(bf16)
+            go(ib2.at[i], ib2r.at[z], i_send.at[1, i], i_recv.at[1, z], (q * 2 + y, f))
+        else:
+            ri[...] = part
+
+    acc = ro[pl.ds(pl.multiple_of(c * rows_out, 8), rows_out), :]
+    for k in range(1, outer):
+        q = lax.rem(z + k, outer)
+        copy(ob2.at[q], ob2r.at[q], o_send.at[k], o_recv.at[1 + q], (q * 2 + y, f)).wait_recv()
+        acc = acc + ob2r[q].astype(f32)
+    acc = acc * (1.0 / root_tokens)
+    ro[:rows_out, :] = acc
+    nout_out[...] = jnp.broadcast_to(jnp.sum(acc * acc, axis=0, keepdims=True), (8, d))
+    for k in range(1, n):
+        go(nout_out, nout_all.at[c], n_send.at[0, k], n_recv.at[0, c], (lax.rem(c + k, n), f))
+    nout_all[c] = nout_out[...]
+
+    gpt = gp[...].T
+    wi = wi_all[...].reshape(cin, d)
+    gh_ref[...] = dot1(gpt, wi, NN).astype(bf16)
+
+    weight = jnp.zeros((1, d), f32)
+    for s in range(n):
+        w = wo_all[s].astype(f32)
+        weight = weight + jnp.sum(w * w, axis=0, keepdims=True)
+    w = win_ref[...].astype(f32)
+    weight_in = jnp.sum(w * w, axis=1, keepdims=True)
+
+    acc = ri[...]
+    for k in range(1, outer):
+        q = lax.rem(z + k, outer)
+        copy(ib2.at[0], ib2r.at[q], i_send.at[1, 0], i_recv.at[1, q], (q * 2 + y, f)).wait_recv()
+        acc = acc + ib2r[q].astype(f32)
+    acc = acc * (1.0 / root_tokens)
+    ri[...] = acc
+    at = lax.broadcasted_iota(jnp.int32, (rows_in, 128), 1)
+    nin_out[...] = jnp.where(at < 64, jnp.sum(acc * acc, axis=1, keepdims=True), weight_in)
+    for k in range(1, fs):
+        go(nin_out, nin_all.at[f], n_send.at[1, k], n_recv.at[1, f], (c, lax.rem(f + k, fs)))
+    nin_all[f] = nin_out[...]
+
+    grad_square = nout_all[c, 0:1, :]
+    for k in range(1, n):
+        s = lax.rem(c + n - k, n)
+        copy(nout_out, nout_all.at[s], n_send.at[0, k], n_recv.at[0, s], (s, f)).wait_recv()
+        grad_square = grad_square + nout_all[s, 0:1, :]
+    factor = jnp.minimum(1.0, clip_output * jnp.maximum(jnp.sqrt(weight), 0.001)
+                         / jnp.maximum(jnp.sqrt(grad_square), 1e-06))
+    gwo_ref[...] = ro[:rows_out, :] * factor
+
+    square = nin_all[f]
+    for k in range(1, fs):
+        p = lax.rem(f + fs - k, fs)
+        copy(nin_out, nin_all.at[p], n_send.at[1, k], n_recv.at[1, p], (c, p)).wait_recv()
+        square = square + nin_all[p]
+    root = jnp.sqrt(square)
+    factor = jnp.minimum(1.0, clip_input * jnp.maximum(root[:, 64:65], 0.001)
+                         / jnp.maximum(root[:, 0:1], 1e-06))
+    gwi_ref[...] = ri[...] * factor
+    for made in sent:
+        made.wait_send()
+
+
+def one_kernel(n, fs, hidden, w_in, decay, norm_gain, w_out, grad_out):
+    tok, d = hidden.shape
+    rows_in, rows_out = w_in.shape[0], w_out.shape[0]
+    cin, hp = rows_in * n, rows_out * n
+    nst = (cin - 2 * hp) // 2
+    hpf, outer = hp // fs, n // 2
+    half = (cin + hp) // 2
+    size = half // PARTS
+    V = pltpu.VMEM
+    dma = pltpu.SemaphoreType.DMA
+    scratch = [
+        V((d, tok), bf16), V((d, tok), bf16), V((n, rows_in, d), bf16), V((n, rows_out, d), bf16),
+        V((cin + hp, tok), f32), V((PARTS, size, tok), f32), V((PARTS, size, tok), bf16),
+        V((PARTS, size, tok), bf16),
+        V((hp, tok), f32), V((hpf + 8, nst), f32), V((n, hpf + 8, nst), f32), V((hp, nst), f32),
+        V((hpf, nst), bf16), V((n, hpf, nst), bf16), V((hp, nst), f32),
+        V((hp, d), f32), V((outer, rows_out, d), bf16), V((outer, rows_out, d), bf16),
+        V((outer, rows_out, d), bf16), V((outer, rows_out, d), bf16),
+        V((cin, tok), bf16), V((rows_in, d), f32),
+        V((outer, rows_in, d), bf16), V((outer, rows_in, d), bf16),
+        V((outer, rows_in, d), bf16), V((outer, rows_in, d), bf16),
+        V((rows_in, 128), f32), V((fs, rows_in, 128), f32), V((8, d), f32), V((n, 8, d), f32),
+        dma((2, n)), dma((2, n)), dma((3, PARTS)), dma((3, PARTS)), dma((4, n)), dma((4, n)),
+        dma((1 + outer,)), dma((1 + outer,)), dma((2, outer)), dma((2, outer)),
+        dma((2, n)), dma((2, n)), V((hp, nst), f32), V((PARTS, size, tok), f32),
+    ]
+    vm = pl.BlockSpec(memory_space=pltpu.VMEM)
+    return pl.pallas_call(
+        functools.partial(fused, n, fs, math.sqrt(tok * n), math.sqrt(d * fs)),
+        out_shape=(
+            jax.ShapeDtypeStruct((tok, d), bf16),
+            jax.ShapeDtypeStruct((rows_in, d), f32),
+            jax.ShapeDtypeStruct((rows_out, d), f32),
+        ),
+        in_specs=[vm] * 6,
+        out_specs=(vm, vm, vm),
+        scratch_shapes=scratch,
+        compiler_params=pltpu.CompilerParams(
+            collective_id=0, has_side_effects=True, vmem_limit_bytes=60 * 1024 * 1024),
+    )(hidden, w_in, decay, norm_gain[:, None], w_out, grad_out)
+
+
 def solution(mesh):
+    n, fs = mesh.shape["ctx"], mesh.shape["fsdp"]
+
+    def body(hidden, w_in, decay, norm_gain, w_out, grad_out):
+        whole_tiles = w_in.shape[0] % 16 == 0 and w_out.shape[0] % 16 == 0
+        if whole_tiles and fs == decay.shape[0] and fs % 2 == 0 and n % 2 == 0 and n >= 4:
+            return one_kernel(n, fs, hidden, w_in, decay, norm_gain, w_out, grad_out)
+        return local(hidden, w_in, decay, norm_gain, w_out, grad_out)
+
     return jax.shard_map(
-        local,
+        body,
         mesh=mesh,
         in_specs=(
             P("ctx", "fsdp"),

time: 383 us -> 120 us (0.31)
  waiting for transfers between devices: 149 us -> 0 us
  blocking collectives: 132 us -> 0 us
  Pallas kernels: 0 us -> 113 us
  matrix products: 43.5 us -> 0 us
  other arithmetic: 26.1 us -> 0 us
  between operations: 14.7 us -> 0.66 us
  local copies, waits for them, and re-layouts: 14.8 us -> 5.47 us
    pallas_call x0 -> x1, Pallas kernels: none -> 113 us  [one_kernel(): pl.pallas_call(functools.partial(fused, n, fs, math.sqrt(tok * n), math.s...]
    reduce_scatter x2 -> x0, waiting for transfers between devices: 87.8 us -> none  [the longest x1 54.6 us: local(): lax.psum_scatter(lax.dot_general(columns, hidden, contract_first, preferr...]
    all_gather x2 -> x0, blocking collectives: 67.3 us -> none  [the longest x1 33.8 us: local(): slab_out = lax.all_gather(w_out, 'ctx', axis=0, tiled=True)]
    psum x1 -> x0, waiting for transfers between devices: 47.7 us -> none  [local(): projection, grad_normed = lax.psum((partial_proj, partial_grad), 'fsdp')]
    dot_general x17 -> x0, matrix products: 43.5 us -> none  [the longest x3 16.2 us: intra_block(): jnp.einsum('hts,shp->thp', mixed, x_heads, precision=highest)]
    unnamed x2 -> x0, blocking collectives: 39 us -> none
    psum x2 -> x0, blocking collectives: 25.9 us -> none  [the longest x1 19.8 us: local(): grad_square = lax.psum(jnp.sum(raw_out * raw_out, axis=0), 'ctx')]
    all_gather x2 -> x0, waiting for transfers between devices: 12.9 us -> none  [the longest x1 12.9 us: local(): lax.all_gather(w_in, 'ctx', axis=0, tiled=True)]
  transfers between devices with their start and end apart: 5 -> 0, of which waited for: 4 -> 0; matrix products, arithmetic and copies ran while one was open for 11% -> 0% of each run, Pallas kernels for 0% -> 0%
where the time goes in v1:
time: 120 us; the launch traced here: 119 us
  Pallas kernels  113 us (94%)
  local copies, waits for them, and re-layouts  5.47 us (5%)
    pallas_call x1, Pallas kernels, one_kernel(): pl.pallas_call(functools.partial(fused, n, fs, math.sqrt(tok * n), math.s...  113 us
    unnamed x9, local copies, waits for them, and re-layouts  4.67 us

profile of v1, /device:TPU:0, one launch (start us, length us, event | category | flops | bytes accessed | tf_op | source)
XLA Modules:
  0.0 119.3 jit_solution(5617097521035221722)
XLA Ops:
  0.6 0.0 copy-start.2
  0.6 0.7 copy-done.2
  1.3 0.8 copy.9.gain_ref
  2.1 113.2 %shard_map.85 = (bf16[512,1024]{1,0:T(8,128)(2,1)}, f32[96,1024]{1,0:T(8,128)}, f32[32,1024]{1,0:T(8,128)}) custom-call(bf16[512,1024]{1,0:T(8,128)(2,1)} %hid_ref.1, bf16[96,1024]{1,0:T(8,128)(2,1)} %win_ref.1, f32[4,512]{1,0:T(4,128)} %dec_ref.1, f32[256,1]{1,0:T(8,128)} %copy.9.gain_ref, bf16[32,1024]{1,0:T(8,128)(2,1)} %wout_ref.1, ...), custom_call_target="tpu_custom_call" | custom-call | tf_op jit(solution)/shard_map/pallas_call | solution.py:530
  115.3 0.0 copy-start
  115.3 2.3 %copy.13 = bf16[512,1024]{1,0:T(8,128)(2,1)} copy(bf16[512,1024]{1,0:T(8,128)(2,1)} %get-tuple-element.6) | data formatting | bytes 2097152
  117.7 0.0 copy-done
  117.7 0.0 copy-start.1
  117.7 0.7 copy.14
  118.4 0.3 copy-done.1
  118.7 0.7 copy.15
Async XLA Ops:
  0.6 0.7 copy-start.2
  115.3 2.3 %copy-start = (f32[96,1024]{1,0:T(8,128)S(1)}, f32[96,1024]{1,0:T(8,128)}, u32[]{:S(2)}) copy-start(f32[96,1024]{1,0:T(8,128)} %get-tuple-element.7) | copy-start | bytes 1179652
  117.7 1.0 copy-start.1

commit v2 on v1

--- a/solution.py
+++ b/solution.py
@@ -196,7 +196,6 @@
 f32 = jnp.float32
 bf16 = jnp.bfloat16
 EPS = 1e-05
-PARTS = 4
 
 
 def split(a):
@@ -220,12 +219,12 @@
     n, fs, root_tokens, clip_input,
     hid_ref, win_ref, dec_ref, gain_ref, wout_ref, gout_ref,
     gh_ref, gwi_ref, gwo_ref,
-    hidT, goutT, wi_all, wo_all, pT, core_in, x_out, x_in,
+    hidT, goutT, wi_all, wo_all, pT, buf, core_in, x_out, x_in, c_in, e_out, e_all,
     e_ref, st_out, st_all, s0_ref, ad_out, ad_all, g_ref,
     ro, ob1, ob1r, ob2, ob2r, gp, ri, ib1, ib1r, ib2, ib2r,
     nin_out, nin_all, nout_out, nout_all,
     g_send, g_recv, p_send, p_recv, s_send, s_recv, o_send, o_recv, i_send, i_recv,
-    n_send, n_recv, tmp, c_in,
+    n_send, n_recv, tmp,
 ):
     c = lax.axis_index("ctx")
     f = lax.axis_index("fsdp")
@@ -249,11 +248,18 @@
 
     sent = []
 
-    def go(*args):
-        made = copy(*args)
-        made.start()
-        sent.append(made)
-        return made
+    def go(*args, when=None):
+        if when is None:
+            copy(*args).start()
+        else:
+            pl.when(when)(lambda: copy(*args).start())
+        sent.append((when, args))
+
+    def arrive(*args, when=None):
+        if when is None:
+            copy(*args).wait_recv()
+        else:
+            pl.when(when)(lambda: copy(*args).wait_recv())
 
     barrier = pltpu.get_barrier_semaphore()
     for k in range(1, n):
@@ -263,13 +269,13 @@
     pl.semaphore_wait(barrier, n + fs - 2)
 
     both = ((win_ref, wi_all), (wout_ref, wo_all))
+    up = jnp.minimum(z + 1, outer - 1) * 2 + y
+    down = jnp.maximum(z - 1, 0) * 2 + y
+    order = [1, outer - 1] + list(range(2, outer - 1))
     for a, (src, dst) in enumerate(both):
-        go(src, dst.at[c], g_send.at[a, 0], g_recv.at[a, c], (yn, f))
-    order = [1, outer - 1] + list(range(2, outer - 1))
-    for k in order:
-        peer = lax.rem(z + k, outer) * 2 + y
-        for a, (src, dst) in enumerate(both):
-            go(src, dst.at[c], g_send.at[a, k], g_recv.at[a, c], (peer, f))
+        go(src, dst.at[c], g_send.at[0, a, c], g_recv.at[a, c], (up, f), when=z < outer - 1)
+        go(src, dst.at[c], g_send.at[1, a, c], g_recv.at[a, c], (down, f), when=z > 0)
+        go(src, dst.at[c], g_send.at[2, a, c], g_recv.at[a, c], (yn, f))
     wi_all[c] = win_ref[...]
     wo_all[c] = wout_ref[...]
     hidT[...] = hid_ref[...].T
@@ -286,48 +292,118 @@
         e_ref[h * (hp // heads) : (h + 1) * (hp // heads), :] = jnp.broadcast_to(
             decay[h : h + 1], (hp // heads, tok))
 
+    e_out[...] = jnp.broadcast_to(
+        e_ref[pl.ds(pl.multiple_of(f * hpf, 8), 8), tok - 128 : tok][:, 127:128], (8, nst))
+    e_all[c] = e_out[...]
+    for k in range(1, n):
+        go(e_out, e_all.at[c], s_send.at[4, k], s_recv.at[4, c], (lax.rem(c + k, n), f))
+
+    hi, ho = rows_in // 2, rows_out // 2
+    half = hi + ho
+    mine = pl.ds(pl.multiple_of(core * half, 8), half)
+    other = pl.ds(pl.multiple_of((1 - core) * half, 8), half)
+
+    def place(s, which, value):
+        pT[pl.ds(pl.multiple_of(s * rows_in + which * hi, 8), hi), :] = value[:hi]
+        pT[pl.ds(pl.multiple_of(cin + s * rows_out + which * ho, 8), ho), :] = value[hi:]
+
+    def to_pair(s):
+        return (buf.at[s, other], core_in.at[s], p_send.at[0, s], p_recv.at[0, s], (c, fcore))
+
+    def across(s):
+        return (x_out.at[s], x_in.at[s], p_send.at[1, s], p_recv.at[1, s], (c, fx))
+
+    def back(s):
+        return (buf.at[s, mine], c_in.at[s], p_send.at[2, s], p_recv.at[2, s], (c, fcore))
+
     def project(s):
-        pT[pl.ds(pl.multiple_of(s * rows_in, 8), rows_in), :] = dot1(wi_all[s], hidT[...], NN)
-        pT[pl.ds(pl.multiple_of(cin + s * rows_out, 8), rows_out), :] = dot1(
-            wo_all[s], goutT[...], NN)
-
-    project(c)
-    for k in order:
-        s = lax.rem(z + outer - k, outer) * 2 + y
+        left = dot1(wi_all[s], hidT[...], NN)
+        right = dot1(wo_all[s], goutT[...], NN)
+        buf[s, :hi] = left[:hi]
+        buf[s, hi:half] = right[:ho]
+        buf[s, half : half + hi] = left[hi:]
+        buf[s, half + hi :] = right[ho:]
+        copy(*to_pair(s)).start()
+
+    def pair_sum(s):
+        copy(*to_pair(s)).wait_recv()
+        total = buf[s, mine] + core_in[s]
+        buf[s, mine] = total
+        x_out[s] = total.astype(bf16)
+        copy(*across(s)).start()
+
+    def full_sum(s):
+        copy(*across(s)).wait_recv()
+        total = buf[s, mine] + x_in[s].astype(f32)
+        buf[s, mine] = total
+        copy(*back(s)).start()
+        place(s, core, total)
+
+    def collect(s):
+        copy(*back(s)).wait_recv()
+        place(s, 1 - core, c_in[s])
+
+    def landed(s, fwd, across_pair):
         for a, (src, dst) in enumerate(both):
-            copy(src, dst.at[s], g_send.at[a, k], g_recv.at[a, s], (yn, f)).wait_recv()
-            go(dst.at[s], dst.at[s], g_send.at[a, outer + k], g_recv.at[a, s], (yn, f))
+            copy(dst.at[s], dst.at[s], g_send.at[2, a, s], g_recv.at[a, s], (yn, f)).wait_recv()
+            if fwd is not None:
+                has, to, way = fwd
+                pl.when(has)(lambda: copy(
+                    dst.at[s], dst.at[s], g_send.at[way, a, s], g_recv.at[a, s], (to, f)).start())
+            if across_pair:
+                copy(dst.at[s], dst.at[s], g_send.at[2, a, s], g_recv.at[a, s], (yn, f)).start()
+
+    def row(k, way):
+        there = z - k if way == 0 else z + k
+        has = there >= 0 if way == 0 else there < outer
+        q = jnp.maximum(there, 0) if way == 0 else jnp.minimum(there, outer - 1)
+        fwd = (z < outer - 1, up, 0) if way == 0 else (z > 0, down, 1)
+        return has, q, fwd
+
+    events = [(None, c, None, False, False)]
+    later = [(None, z * 2 + 1 - y, None, True, False)]
+    for k in range(1, outer):
+        for way in (0, 1):
+            has, q, fwd = row(k, way)
+            events.append((has, q * 2 + y, fwd, True, True))
+        events.extend(later)
+        later = []
+        for way in (0, 1):
+            has, q, fwd = row(k, way)
+            later.append((has, q * 2 + 1 - y, None, True, False))
+    events.extend(later)
+
+    def under(has, fn, *args):
+        if has is None:
+            fn(*args)
+        else:
+            pl.when(has)(lambda: fn(*args))
+
+    def take(s, fwd, wait, across_pair):
+        if wait:
+            landed(s, fwd, across_pair)
         project(s)
-    for k in [0] + order:
-        s = lax.rem(z + outer - k, outer) * 2 + 1 - y
+
+    def release(s, fwd, across_pair):
+        for args in (to_pair(s), across(s), back(s)):
+            copy(*args).wait_send()
         for a, (src, dst) in enumerate(both):
-            copy(src, dst.at[s], g_send.at[a, 0], g_recv.at[a, s], (yn, f)).wait_recv()
-        project(s)
-
-    half = (cin + hp) // 2
-    size = half // PARTS
-    first = []
-    for j in range(PARTS):
-        part = pl.ds(pl.multiple_of((1 - core) * half + j * size, 8), size)
-        first.append(copy(pT.at[part], core_in.at[j], p_send.at[0, j], p_recv.at[0, j], (c, fcore)))
-        first[j].start()
-    mine = [pl.ds(pl.multiple_of(core * half + j * size, 8), size) for j in range(PARTS)]
-    for j in range(PARTS):
-        copy(core_in.at[j], core_in.at[j], p_send.at[0, j], p_recv.at[0, j], (c, fcore)).wait_recv()
-        total = pT[mine[j], :] + core_in[j]
-        pT[mine[j], :] = total
-        x_out[j] = total.astype(bf16)
-        go(x_out.at[j], x_in.at[j], p_send.at[1, j], p_recv.at[1, j], (c, fx))
-    for j in range(PARTS):
-        copy(x_out.at[j], x_in.at[j], p_send.at[1, j], p_recv.at[1, j], (c, fx)).wait_recv()
-        pT[mine[j], :] = pT[mine[j], :] + x_in[j].astype(f32)
-        go(pT.at[mine[j]], c_in.at[j], p_send.at[2, j], p_recv.at[2, j], (c, fcore))
-    for j in range(PARTS):
-        first[j].wait_send()
-    for j in range(PARTS):
-        part = pl.ds(pl.multiple_of((1 - core) * half + j * size, 8), size)
-        copy(c_in.at[j], c_in.at[j], p_send.at[2, j], p_recv.at[2, j], (c, fcore)).wait_recv()
-        pT[part, :] = c_in[j]
+            def there(way, to):
+                copy(dst.at[s], dst.at[s], g_send.at[way, a, s], g_recv.at[a, s],
+                     (to, f)).wait_send()
+            if fwd is not None:
+                under(fwd[0], there, fwd[2], fwd[1])
+            if across_pair:
+                there(2, yn)
+
+    total_events = len(events)
+    for i in range(total_events + 5):
+        if i < total_events:
+            has, s, fwd, wait, across_pair = events[i]
+            under(has, take, s, fwd, wait, across_pair)
+        for lag, fn in ((1, pair_sum), (3, full_sum), (5, collect)):
+            if 0 <= i - lag < total_events:
+                under(events[i - lag][0], fn, events[i - lag][1])
 
     e = e_ref[...]
     einv = 1.0 / e
@@ -339,12 +415,10 @@
     xs2, b2, c2 = split(xs), split(bT), split(cT)
     tmp[...] = dot3(xs2, b2, NT) * eend
     own = pl.ds(pl.multiple_of(f * hpf, 8), hpf)
-    st_out[:hpf, :] = tmp[own, :]
-    last = e_ref[pl.ds(pl.multiple_of(f * hpf, 8), 8), tok - 128 : tok]
-    st_out[hpf:, :] = jnp.broadcast_to(last[:, 127:128], (8, nst))
-    for k in range(1, n):
-        go(st_out, st_all.at[c], s_send.at[0, k], s_recv.at[0, c], (lax.rem(c + k, n), f))
-    st_all[c] = st_out[...]
+    st_out[...] = tmp[own, :]
+    for k in range(n - 1, 0, -1):
+        go(st_out, st_all.at[c], s_send.at[0, k], s_recv.at[0, c],
+           (jnp.minimum(c + k, n - 1), f), when=c + k < n)
 
     upper = lax.broadcasted_iota(jnp.int32, (tok, tok), 0) <= lax.broadcasted_iota(
         jnp.int32, (tok, tok), 1)
@@ -355,10 +429,12 @@
 
     for k in range(1, n):
         s = lax.rem(c + n - k, n)
-        copy(st_out, st_all.at[s], s_send.at[0, k], s_recv.at[0, s], (s, f)).wait_recv()
+        arrive(e_out, e_all.at[s], s_send.at[4, k], s_recv.at[4, s], (s, f))
+        s = jnp.maximum(c - k, 0)
+        arrive(st_out, st_all.at[s], s_send.at[0, k], s_recv.at[0, s], (s, f), when=c - k >= 0)
     state = jnp.zeros((hpf, nst), f32)
     for k in range(n - 1):
-        new = st_all[k, hpf : hpf + 1, :] * state + st_all[k, :hpf, :]
+        new = e_all[k, 0:1, :] * state + st_all[k]
         state = jnp.where(k < c, new, state)
     s0_ref[own, :] = state
     for k in range(1, fs):
@@ -379,9 +455,9 @@
     dys2 = split(dgated * silu * e)
     tmp[...] = dot3(dys2, c2, NT)
     ad_out[...] = tmp[own, :].astype(bf16)
-    for k in range(1, n):
-        go(ad_out, ad_all.at[c], s_send.at[2, k], s_recv.at[2, c], (lax.rem(c + k, n), f))
-    ad_all[c] = ad_out[...]
+    for k in range(n - 1, 0, -1):
+        go(ad_out, ad_all.at[c], s_send.at[2, k], s_recv.at[2, c],
+           (jnp.maximum(c - k, 0), f), when=c - k >= 0)
     gp[:hp, :] = (dgated * yT * (sig * (1.0 + gate * (1.0 - sig)))).astype(bf16)
 
     ro[...] = dot1(normed, gout_ref[...], NN)
@@ -403,11 +479,11 @@
         ob2[q] = total.astype(bf16)
 
     for k in range(1, n):
-        s = lax.rem(c + n - k, n)
-        copy(ad_out, ad_all.at[s], s_send.at[2, k], s_recv.at[2, s], (s, f)).wait_recv()
+        s = jnp.minimum(c + k, n - 1)
+        arrive(ad_out, ad_all.at[s], s_send.at[2, k], s_recv.at[2, s], (s, f), when=c + k < n)
     adj = jnp.zeros((hpf, nst), f32)
     for k in range(n - 1, 0, -1):
-        new = st_all[k, hpf : hpf + 1, :] * adj + ad_all[k].astype(f32)
+        new = e_all[k, 0:1, :] * adj + ad_all[k].astype(f32)
         adj = jnp.where(k > c, new, adj)
     g_ref[own, :] = adj
     for k in range(1, fs):
@@ -496,8 +572,10 @@
     factor = jnp.minimum(1.0, clip_input * jnp.maximum(root[:, 64:65], 0.001)
                          / jnp.maximum(root[:, 0:1], 1e-06))
     gwi_ref[...] = ri[...] * factor
-    for made in sent:
-        made.wait_send()
+    for has, args in sent:
+        under(has, lambda args: copy(*args).wait_send(), args)
+    for has, s, fwd, wait, across_pair in events:
+        under(has, release, s, fwd, across_pair)
 
 
 def one_kernel(n, fs, hidden, w_in, decay, norm_gain, w_out, grad_out):
@@ -506,15 +584,15 @@
     cin, hp = rows_in * n, rows_out * n
     nst = (cin - 2 * hp) // 2
     hpf, outer = hp // fs, n // 2
-    half = (cin + hp) // 2
-    size = half // PARTS
+    half = (rows_in + rows_out) // 2
     V = pltpu.VMEM
     dma = pltpu.SemaphoreType.DMA
     scratch = [
         V((d, tok), bf16), V((d, tok), bf16), V((n, rows_in, d), bf16), V((n, rows_out, d), bf16),
-        V((cin + hp, tok), f32), V((PARTS, size, tok), f32), V((PARTS, size, tok), bf16),
-        V((PARTS, size, tok), bf16),
-        V((hp, tok), f32), V((hpf + 8, nst), f32), V((n, hpf + 8, nst), f32), V((hp, nst), f32),
+        V((cin + hp, tok), f32), V((n, 2 * half, tok), f32), V((n, half, tok), f32),
+        V((n, half, tok), bf16), V((n, half, tok), bf16), V((n, half, tok), f32),
+        V((8, nst), f32), V((n, 8, nst), f32),
+        V((hp, tok), f32), V((hpf, nst), f32), V((n, hpf, nst), f32), V((hp, nst), f32),
         V((hpf, nst), bf16), V((n, hpf, nst), bf16), V((hp, nst), f32),
         V((hp, d), f32), V((outer, rows_out, d), bf16), V((outer, rows_out, d), bf16),
         V((outer, rows_out, d), bf16), V((outer, rows_out, d), bf16),
@@ -522,9 +600,9 @@
         V((outer, rows_in, d), bf16), V((outer, rows_in, d), bf16),
         V((outer, rows_in, d), bf16), V((outer, rows_in, d), bf16),
         V((rows_in, 128), f32), V((fs, rows_in, 128), f32), V((8, d), f32), V((n, 8, d), f32),
-        dma((2, n)), dma((2, n)), dma((3, PARTS)), dma((3, PARTS)), dma((4, n)), dma((4, n)),
+        dma((3, 2, n)), dma((2, n)), dma((3, n)), dma((3, n)), dma((5, n)), dma((5, n)),
         dma((1 + outer,)), dma((1 + outer,)), dma((2, outer)), dma((2, outer)),
-        dma((2, n)), dma((2, n)), V((hp, nst), f32), V((PARTS, size, tok), f32),
+        dma((2, n)), dma((2, n)), V((hp, nst), f32),
     ]
     vm = pl.BlockSpec(memory_space=pltpu.VMEM)
     return pl.pallas_call(

time: 120 us -> 107 us (0.89)
  Pallas kernels: 113 us -> 100 us
    pallas_call x1, Pallas kernels: 113 us -> 100 us  [one_kernel(): pl.pallas_call(functools.partial(fused, n, fs, math.sqrt(tok * n), math.s...]
where the time goes in v2:
time: 107 us; the launch traced here: 106 us
  Pallas kernels  100 us (93%)
  local copies, waits for them, and re-layouts  5.47 us (5%)
    pallas_call x1, Pallas kernels, one_kernel(): pl.pallas_call(functools.partial(fused, n, fs, math.sqrt(tok * n), math.s...  100 us
    unnamed x9, local copies, waits for them, and re-layouts  4.67 us

profile of v2, /device:TPU:0, one launch (start us, length us, event | category | flops | bytes accessed | tf_op | source)
XLA Modules:
  0.0 106.2 jit_solution(17799134148626644495)
XLA Ops:
  0.6 0.0 copy-start.2
  0.6 0.7 copy-done.2
  1.3 0.8 copy.9.gain_ref
  2.1 100.1 %shard_map.85 = (bf16[512,1024]{1,0:T(8,128)(2,1)}, f32[96,1024]{1,0:T(8,128)}, f32[32,1024]{1,0:T(8,128)}) custom-call(bf16[512,1024]{1,0:T(8,128)(2,1)} %hid_ref.1, bf16[96,1024]{1,0:T(8,128)(2,1)} %win_ref.1, f32[4,512]{1,0:T(4,128)} %dec_ref.1, f32[256,1]{1,0:T(8,128)} %copy.9.gain_ref, bf16[32,1024]{1,0:T(8,128)(2,1)} %wout_ref.1, ...), custom_call_target="tpu_custom_call" | custom-call | tf_op jit(solution)/shard_map/pallas_call | solution.py:608
  102.2 0.0 copy-start
  102.2 2.3 %copy.13 = bf16[512,1024]{1,0:T(8,128)(2,1)} copy(bf16[512,1024]{1,0:T(8,128)(2,1)} %get-tuple-element.6) | data formatting | bytes 2097152
  104.6 0.0 copy-done
  104.6 0.0 copy-start.1
  104.6 0.7 copy.14
  105.3 0.3 copy-done.1
  105.6 0.7 copy.15
Async XLA Ops:
  0.6 0.7 copy-start.2
  102.2 2.3 %copy-start = (f32[96,1024]{1,0:T(8,128)S(1)}, f32[96,1024]{1,0:T(8,128)}, u32[]{:S(2)}) copy-start(f32[96,1024]{1,0:T(8,128)} %get-tuple-element.7) | copy-start | bytes 1179652
  104.6 1.0 copy-start.1

commit v3 on v2

--- a/solution.py
+++ b/solution.py
@@ -466,10 +466,10 @@
         ob1[q] = ro[at, :].astype(bf16)
     go(ob1, ob1r, o_send.at[0], o_recv.at[0], (yn, f))
 
-    dscores2 = split(jnp.where(upper, dot3(transposed(xs2), dys2, NN), 0.0))
-    gp[2 * hp + nst :, :] = (dot3(b2, dscores2, NN) + dot3(transposed(s02), dys2, NN)).astype(bf16)
-    db = dot3(c2, dscores2, NT)
-    dxs = dot3(dys2, scores2, NT)
+    dscores = jnp.where(upper, dot1(xs2[0].T, dys2[0], NN), 0.0).astype(bf16)
+    gp[2 * hp + nst :, :] = (dot1(b2[0], dscores, NN) + dot3(transposed(s02), dys2, NN)).astype(bf16)
+    db = dot1(c2[0], dscores, NT)
+    dxs = dot1(dys2[0], scores2[0], NT)
 
     copy(ob1, ob1r, o_send.at[0], o_recv.at[0], (yn, f)).wait_recv()
     for q in range(outer):

time: 107 us -> 107 us (level)
  no operation moved by 1% of the time
where the time goes in v3:
time: 107 us; the launch traced here: 106 us
  Pallas kernels  99.4 us (93%)
  local copies, waits for them, and re-layouts  5.47 us (5%)
    pallas_call x1, Pallas kernels, one_kernel(): pl.pallas_call(functools.partial(fused, n, fs, math.sqrt(tok * n), math.s...  99.4 us
    unnamed x9, local copies, waits for them, and re-layouts  4.67 us

profile of v3, /device:TPU:0, one launch (start us, length us, event | category | flops | bytes accessed | tf_op | source)
XLA Modules:
  0.0 105.6 jit_solution(10499435448291487900)
XLA Ops:
  0.6 0.0 copy-start.2
  0.6 0.7 copy-done.2
  1.3 0.8 copy.9.gain_ref
  2.1 99.4 %shard_map.85 = (bf16[512,1024]{1,0:T(8,128)(2,1)}, f32[96,1024]{1,0:T(8,128)}, f32[32,1024]{1,0:T(8,128)}) custom-call(bf16[512,1024]{1,0:T(8,128)(2,1)} %hid_ref.1, bf16[96,1024]{1,0:T(8,128)(2,1)} %win_ref.1, f32[4,512]{1,0:T(4,128)} %dec_ref.1, f32[256,1]{1,0:T(8,128)} %copy.9.gain_ref, bf16[32,1024]{1,0:T(8,128)(2,1)} %wout_ref.1, ...), custom_call_target="tpu_custom_call" | custom-call | tf_op jit(solution)/shard_map/pallas_call | solution.py:608
  101.6 0.0 copy-start
  101.6 2.3 %copy.13 = bf16[512,1024]{1,0:T(8,128)(2,1)} copy(bf16[512,1024]{1,0:T(8,128)(2,1)} %get-tuple-element.6) | data formatting | bytes 2097152
  103.9 0.0 copy-done
  103.9 0.0 copy-start.1
  103.9 0.7 copy.14
  104.6 0.3 copy-done.1
  104.9 0.7 copy.15
Async XLA Ops:
  0.6 0.7 copy-start.2
  101.6 2.3 %copy-start = (f32[96,1024]{1,0:T(8,128)S(1)}, f32[96,1024]{1,0:T(8,128)}, u32[]{:S(2)}) copy-start(f32[96,1024]{1,0:T(8,128)} %get-tuple-element.7) | copy-start | bytes 1179652
  103.9 1.0 copy-start.1
